TPU v7x, 256 devices: a whole 4x4x8 slice. The times are simulated.
256 devices in a mesh: expert: 64 (over z, y, core), replica: 4 (over x).
Axes of the slice: x: 4, y: 4, z: 8, core: 2. Of those that a mesh axis runs over, the one named last changes fastest.
Arguments:
- hidden_first: bfloat16 [2048, 4096], P(('expert', 'replica')), may hold values from -40 to 40
- hidden_second: bfloat16 [2048, 4096], P(('expert', 'replica')), may hold values from -40 to 40
- routes_first: int32 [2048, 8], P(('expert', 'replica')), may hold values from 0 to 63, all different within a row; in each aligned block of 8 rows (0 to 7, 8 to 15, ...) at most 2 rows name the same one
- routes_second: int32 [2048, 8], P(('expert', 'replica')), may hold values from 0 to 63, all different within a row; in each aligned block of 8 rows (0 to 7, 8 to 15, ...) at most 2 rows name the same one
- mixing_first: float32 [2048, 8], P(('expert', 'replica')), may hold values from 0.05 to 0.5
- mixing_second: float32 [2048, 8], P(('expert', 'replica')), may hold values from 0.05 to 0.5
- norm_gain: float32 [4096], replicated, may hold values from 0.1 to 1.9
- expert_owner: int32 [64], replicated, may hold values from 0 to 63, each once
- swap_flags: int32 [64], replicated, may hold values from 0 to 1, as said below
- gate_up_values: bfloat16 [64, 2, 4096, 1024], P('expert', None, None, 'replica'), may hold values from -0.09375 to 0.09375
- gate_up_scales: bfloat16 [64, 2, 32, 8], P('expert', None, None, 'replica'), may hold values from 0.5 to 2
- down_values: bfloat16 [64, 1024, 4096], P('expert', 'replica'), may hold values from -0.1875 to 0.1875
- down_scales: bfloat16 [64, 8, 32], P('expert', 'replica'), may hold values from 0.5 to 2
Outputs:
- output_first: bfloat16 [2048, 4096], P(('expert', 'replica'))
- output_second: bfloat16 [2048, 4096], P(('expert', 'replica'))
- gate_up_moved: bfloat16 [64, 2, 4096, 1024], P('expert', None, None, 'replica')
- gate_up_scales_moved: bfloat16 [64, 2, 32, 8], P('expert', None, None, 'replica')
- down_moved: bfloat16 [64, 1024, 4096], P('expert', 'replica')
- down_scales_moved: bfloat16 [64, 8, 32], P('expert', 'replica')
Inputs may be any that keep to these rules, and one draw needn't show every extreme that they name: swap_flags[d] equals swap_flags[(d + 32) mod 64].
All inputs are finite; a program needn't handle non-finite values.
Results may differ from a plain program's by a relative error of at most 0.012.
Values may be sent and summed in bfloat16 or wider, within the bound.
No kernel may reach another device: no remote copies, remote signals or barrier semaphores. Data moves between devices by JAX's collectives and lax.ppermute only.
A program may use at most 128 MiB of HBM per device.

v0:
```python
import jax
import jax.numpy as jnp
from jax import lax
from jax.sharding import PartitionSpec as P


def partner(block, axis, bit):
    count = lax.axis_size(axis)
    route = []
    for low in range(count):
        high = low | 1 << bit
        if high != low and high < count:
            route += [(low, high), (high, low)]
    return lax.ppermute(block, axis, route)


def dequantize(values, scales):
    height, breadth = (values.shape[-2], values.shape[-1])
    block_rows, block_cols = (scales.shape[-2], scales.shape[-1])
    leading = values.shape[:-2]
    blocked = values.astype(jnp.float32).reshape(
        leading + (block_rows, height // block_rows, block_cols, breadth // block_cols)
    )
    scaled = blocked * scales.astype(jnp.float32)[..., :, None, :, None]
    return scaled.reshape(values.shape).astype(jnp.bfloat16)


def rms_normed(hidden, norm_gain):
    widened = hidden.astype(jnp.float32)
    inverse_rms = lax.rsqrt(jnp.mean(widened * widened, axis=-1, keepdims=True) + 1e-06)
    return (widened * inverse_rms * norm_gain).astype(jnp.bfloat16)


def rounded(partial_sum):
    return lax.optimization_barrier(partial_sum.astype(jnp.bfloat16)).astype(jnp.float32)


def expert_partial(token_rows, weights):
    gate_up, down_proj = weights
    gate_act = jnp.dot(token_rows, gate_up[0], preferred_element_type=jnp.float32)
    up_act = jnp.dot(token_rows, gate_up[1], preferred_element_type=jnp.float32)
    inner_act = (jax.nn.silu(gate_act) * up_act).astype(jnp.bfloat16)
    return rounded(jnp.dot(inner_act, down_proj, preferred_element_type=jnp.float32))


def pick_slots(routes, owner_slots, experts, capacity):
    tokens_here, top_count = routes.shape
    expert_ids = jnp.arange(owner_slots.shape[0], dtype=jnp.int32)
    target = jnp.sum(jnp.where(routes[:, :, None] == expert_ids, owner_slots, 0), axis=-1).reshape(
        -1
    )
    device_ids = jnp.arange(experts, dtype=jnp.int32)
    target_hot = (target[:, None] == device_ids).astype(jnp.int32)
    earlier = jnp.cumsum(target_hot, axis=0) - target_hot
    rank_in = jnp.sum(earlier * target_hot, axis=1)
    slot_ids = target * capacity + rank_in
    columns = jnp.arange(experts * capacity, dtype=jnp.int32)
    return (
        (slot_ids[:, None] == columns)
        .astype(jnp.float32)
        .reshape(tokens_here, top_count, experts * capacity)
    )


def finish(partial_terms):
    summed = lax.psum_scatter(
        partial_terms.astype(jnp.bfloat16), "replica", scatter_dimension=0, tiled=True
    )
    return lax.all_to_all(summed, "expert", split_axis=1, concat_axis=1, tiled=True)


def decode_step(hidden, routes, mixing, norm_gain, owner_slots, weights):
    experts = lax.axis_size("expert")
    copies = lax.axis_size("replica")
    tokens_here, top_count = routes.shape
    features = hidden.shape[1]
    capacity = min(tokens_here, max(2, 2 * tokens_here * top_count // experts))
    normed = rms_normed(hidden, norm_gain)
    own_picks = pick_slots(routes, owner_slots, experts, capacity)
    pooled, pooled_routes = (
        lax.all_gather(normed, "replica", axis=0, tiled=True),
        lax.all_gather(routes, "replica", axis=0, tiled=True),
    )
    grouped = pooled_routes.reshape(copies, tokens_here, top_count)
    pick_table = jax.vmap(
        lambda route_group: pick_slots(route_group, owner_slots, experts, capacity)
    )(grouped)
    placing = jnp.sum(pick_table, axis=2).astype(jnp.bfloat16)
    outgoing = jnp.einsum(
        "rts,rtd->rsd",
        placing,
        pooled.reshape(copies, tokens_here, features),
        preferred_element_type=jnp.float32,
    )
    outgoing = outgoing.astype(jnp.bfloat16).reshape(copies, experts, capacity, features)
    arrived = lax.all_to_all(outgoing, "expert", split_axis=1, concat_axis=1, tiled=True)
    slot_count = arrived.shape[2]
    flat_rows = arrived.reshape(-1, features)
    partial_terms = expert_partial(flat_rows, weights).reshape(
        copies, experts, slot_count, features
    )
    returned = finish(partial_terms)
    mixing_matrix = jnp.einsum("tks,tk->ts", own_picks, mixing, precision=lax.Precision.HIGHEST)
    merged = jnp.dot(
        mixing_matrix,
        returned.reshape(experts * capacity, features).astype(jnp.float32),
        precision=lax.Precision.HIGHEST,
    )
    return merged.astype(jnp.bfloat16)


def body(
    hidden_first,
    hidden_second,
    routes_first,
    routes_second,
    mixing_first,
    mixing_second,
    norm_gain,
    expert_owner,
    swap_flags,
    gate_up_values,
    gate_up_scales,
    down_values,
    down_scales,
):
    experts = lax.axis_size("expert")
    halfway = experts // 2
    my_slot = lax.axis_index("expert")
    current = (gate_up_values, gate_up_scales, down_values, down_scales)
    incoming = partner(
        (gate_up_values, gate_up_scales, down_values, down_scales),
        "expert",
        experts.bit_length() - 2,
    )
    slot_ids = jnp.arange(experts, dtype=jnp.int32)
    flagged = jnp.sum(jnp.where(slot_ids == my_slot, swap_flags, 0)) == 1
    moved_arrays = tuple(
        (
            jnp.where(flagged, fresh_piece, stale_piece)
            for fresh_piece, stale_piece in zip(incoming, current)
        )
    )
    weights_before = (
        dequantize(gate_up_values[0], gate_up_scales[0]),
        dequantize(down_values[0], down_scales[0]),
    )
    output_first = decode_step(
        hidden_first, routes_first, mixing_first, norm_gain, expert_owner, weights_before
    )
    owner_flags = jnp.sum(jnp.where(expert_owner[:, None] == slot_ids, swap_flags, 0), axis=1)
    owner_after = jnp.where(owner_flags == 1, (expert_owner + halfway) % experts, expert_owner)
    weights_after = (
        dequantize(moved_arrays[0][0], moved_arrays[1][0]),
        dequantize(moved_arrays[2][0], moved_arrays[3][0]),
    )
    output_second = decode_step(
        hidden_second, routes_second, mixing_second, norm_gain, owner_after, weights_after
    )
    return (
        output_first,
        output_second,
        moved_arrays[0],
        moved_arrays[1],
        moved_arrays[2],
        moved_arrays[3],
    )


def solution(mesh):
    return jax.shard_map(
        body,
        mesh=mesh,
        in_specs=(
            P(("expert", "replica"), None),
            P(("expert", "replica"), None),
            P(("expert", "replica"), None),
            P(("expert", "replica"), None),
            P(("expert", "replica"), None),
            P(("expert", "replica"), None),
            P(),
            P(),
            P(),
            P("expert", None, None, "replica"),
            P("expert", None, None, "replica"),
            P("expert", "replica", None),
            P("expert", "replica", None),
        ),
        out_specs=(
            P(("expert", "replica"), None),
            P(("expert", "replica"), None),
            P("expert", None, None, "replica"),
            P("expert", None, None, "replica"),
            P("expert", "replica", None),
            P("expert", "replica", None),
        ),
        check_vma=False,
    )
```

profile of v0, /device:TPU:1, one launch (start us, length us, event | category | flops | bytes accessed | tf_op | source)
XLA Modules:
  0.0 738.2 jit_solution(4624766096503249148)
XLA Ops:
  8.7 10.4 %all_gather.14 = s32[32,8]{1,0:T(8,128)S(1)} all-gather(s32[8,8]{1,0:T(8,128)} %param.16), channel_id=1, replica_groups=mesh['expert'=64,'replica'=4] {'replica'}, dimensions={0}, use_global_device_ids=true | all-gather | bytes 1280 | tf_op jit(solution)/shard_map/all_gather | solution.py:82
  20.6 1.0 fusion.23
  21.6 1.0 fusion.26
  22.6 1.0 fusion.28
  23.6 9.4 %all_gather.15 = bf16[32,4096]{1,0:T(8,128)(2,1)S(1)} all-gather(bf16[8,4096]{1,0:T(8,128)(2,1)S(1)} %get-tuple-element.13), channel_id=1, replica_groups=mesh['expert'=64,'replica'=4] {'replica'}, dimensions={0}, use_global_device_ids=true | all-gather | bytes 327680 | tf_op jit(solution)/shard_map/all_gather | solution.py:81
  33.0 3.3 convolution_convert_fusion.1
  36.3 7.6 %reshape.189 = bf16[4,64,2,4096]{3,2,1,0:T(2,128)(2,1)} reshape(bf16[4,128,4096]{2,1,0:T(8,128)(2,1)} %convolution_convert_fusion.1) | data formatting | bytes 8388608 | tf_op jit(solution)/shard_map/reshape | solution.py:95
  43.9 10.2 %copy.44 = bf16[4,64,2,4096]{3,2,0,1:T(2,128)(2,1)} copy(bf16[4,64,2,4096]{3,2,1,0:T(2,128)(2,1)} %reshape.189) | data formatting | bytes 8388608 | tf_op jit(solution)/shard_map/reshape | solution.py:95
  54.1 18.4 %all-to-all-start.2 = ((bf16[4,64,2,4096]{3,2,0,1:T(2,128)(2,1)}), bf16[4,64,2,4096]{3,2,0,1:T(2,128)(2,1)}, u32[]{:S(2)}, u32[]{:S(2)}) async-start(bf16[4,64,2,4096]{3,2,0,1:T(2,128)(2,1)} %copy.44), calls=%async_computation.3 | async-start | bytes 8388608 | tf_op jit(solution)/shard_map/all_to_all | solution.py:96
  72.6 5.5 collective-permute-start
  78.2 5.3 collective-permute-start.1
  83.5 10.1 %all_gather.12 = s32[32,8]{1,0:T(8,128)S(1)} all-gather(s32[8,8]{1,0:T(8,128)S(1)} %copy-done.4), channel_id=1, replica_groups=mesh['expert'=64,'replica'=4] {'replica'}, dimensions={0}, use_global_device_ids=true | all-gather | bytes 1280 | tf_op jit(solution)/shard_map/all_gather | solution.py:82
  94.9 10.6 %all_gather.13 = bf16[32,4096]{1,0:T(8,128)(2,1)S(1)} all-gather(bf16[8,4096]{1,0:T(8,128)(2,1)S(1)} %get-tuple-element.14), channel_id=1, replica_groups=mesh['expert'=64,'replica'=4] {'replica'}, dimensions={0}, use_global_device_ids=true | all-gather | bytes 327680 | tf_op jit(solution)/shard_map/all_gather | solution.py:81
  105.6 3.3 convolution_convert_fusion.3
  108.9 7.8 %reshape.185 = bf16[4,64,2,4096]{3,2,1,0:T(2,128)(2,1)} reshape(bf16[4,128,4096]{2,1,0:T(8,128)(2,1)} %convolution_convert_fusion.3) | data formatting | bytes 8388608 | tf_op jit(solution)/shard_map/reshape | solution.py:95
  116.8 10.2 %copy.39 = bf16[4,64,2,4096]{3,2,0,1:T(2,128)(2,1)} copy(bf16[4,64,2,4096]{3,2,1,0:T(2,128)(2,1)} %reshape.185) | data formatting | bytes 8388608 | tf_op jit(solution)/shard_map/reshape | solution.py:95
  128.2 243.6 %collective-permute-done.3 = bf16[1,2,32]{2,1,0:T(2,128)(2,1)S(1)} collective-permute-done((bf16[1,2,32]{2,1,0:T(2,128)(2,1)S(1)}, bf16[1,2,32]{2,1,0:T(2,128)(2,1)S(1)}, u32[]{:S(2)}, u32[]{:S(2)}) %collective-permute-start.3) | collective-permute-done | bytes 160 | tf_op jit(solution)/shard_map/ppermute | solution.py:14
  373.0 5.4 mul.142
  378.5 11.5 %mul.143 = f32[2,4096,256]{2,1,0:T(8,128)} reshape(f32[2,32,128,2,128]{4,3,2,1,0:T(2,128)} %mul.142) | data formatting | bytes 16777216 | tf_op jit(solution)/shard_map/mul | solution.py:24
  390.0 5.4 mul.158
  395.5 11.5 %mul.159 = f32[2,4096,256]{2,1,0:T(8,128)} reshape(f32[2,32,128,2,128]{4,3,2,1,0:T(2,128)} %mul.158) | data formatting | bytes 16777216 | tf_op jit(solution)/shard_map/mul | solution.py:24
  407.0 1.7 broadcast_select_fusion.1
  408.7 1.3 copy-done.2
  409.9 10.6 %fusion = (bf16[2,4096,256]{2,1,0:T(8,128)(2,1)}, bf16[1,2,4096,256]{3,2,1,0:T(8,128)(2,1)}, bf16[2,4096,256]{2,1,0:T(8,128)(2,1)}) fusion(f32[2,4096,256]{2,1,0:T(8,128)} %mul.159, bf16[1,2,4096,256]{3,2,1,0:T(8,128)(2,1)} %collective-permute-done, bf16[1,2,4096,256]{3,2,1,0:T(8,128)(2,1)S(1)} %copy-done.2, pred[]{:T(512)S(6)} %eq.251, f32[2,4096,256]{2,1,0:T(8,128)} %mul.143), kind=kLoop, calls=%fused_computation.1 | loop fusion | flops 14680064 | bytes 37748736 | tf_op jit(solution)/shard_map/convert_element_type | solution.py:25
  420.5 75.5 %all-to-all-start = ((bf16[4,64,2,4096]{3,2,0,1:T(2,128)(2,1)}), bf16[4,64,2,4096]{3,2,0,1:T(2,128)(2,1)}, u32[]{:S(2)}, u32[]{:S(2)}) async-start(bf16[4,64,2,4096]{3,2,0,1:T(2,128)(2,1)} %copy.39), calls=%async_computation | async-start | bytes 8388608 | tf_op jit(solution)/shard_map/all_to_all | solution.py:96
  496.0 9.7 %copy.45 = bf16[4,64,2,4096]{3,2,1,0:T(2,128)(2,1)} copy(bf16[4,64,2,4096]{3,2,0,1:T(2,128)(2,1)} %all-to-all-done.2) | data formatting | bytes 8388608 | tf_op jit(solution)/shard_map/all_to_all | solution.py:96
  505.8 7.4 reshape.190
  513.1 4.1 fusion.6
  517.2 2.6 mul.163
  519.8 11.9 %convolution_convert_fusion = bf16[512,4096]{1,0:T(8,128)(2,1)} fusion(f32[32,8,32,128]{3,2,1,0:T(8,128)} %bitcast.101, bf16[1,256,4096]{2,1,0:T(8,128)(2,1)} %broadcast_select_fusion.1, f32[512,256]{1,0:T(8,128)S(1)} %fusion.6, bf16[512,4096]{1,0:T(8,128)(2,1)} %reshape.190, bf16[2,4096,256]{2,1,0:T(8,128)(2,1)} %get-tuple-element.6), kind=kOutput, calls=%fused_computation.4 | convolution fusion | flops 2153512960 | bytes 17301504 | tf_op jit(solution)/shard_map/dot_general | solution.py:43
  531.7 7.6 %convert_element_type.200 = bf16[4,64,2,4096]{3,2,1,0:T(2,128)(2,1)} reshape(bf16[512,4096]{1,0:T(8,128)(2,1)} %convolution_convert_fusion) | data formatting | bytes 8388608 | tf_op jit(solution)/shard_map/convert_element_type | solution.py:67
  539.4 7.1 copy.47
  546.5 44.4 %all-to-all-done = bf16[4,64,2,4096]{3,2,0,1:T(2,128)(2,1)} async-done(((bf16[4,64,2,4096]{3,2,0,1:T(2,128)(2,1)}), bf16[4,64,2,4096]{3,2,0,1:T(2,128)(2,1)}, u32[]{:S(2)}, u32[]{:S(2)}) %all-to-all-start) | async-done | bytes 4194336 | tf_op jit(solution)/shard_map/all_to_all | solution.py:96
  590.9 9.7 %copy.40 = bf16[4,64,2,4096]{3,2,1,0:T(2,128)(2,1)} copy(bf16[4,64,2,4096]{3,2,0,1:T(2,128)(2,1)} %all-to-all-done) | data formatting | bytes 8388608 | tf_op jit(solution)/shard_map/all_to_all | solution.py:96
  600.6 7.4 %reshape.186 = bf16[512,4096]{1,0:T(8,128)(2,1)} reshape(bf16[4,64,2,4096]{3,2,1,0:T(2,128)(2,1)} %copy.40) | data formatting | bytes 8388608 | tf_op jit(solution)/shard_map/reshape | solution.py:98
  608.0 4.1 fusion.9
  612.1 2.6 mul.147
  614.7 11.4 %convolution_convert_fusion.2 = bf16[512,4096]{1,0:T(8,128)(2,1)} fusion(f32[32,8,32,128]{3,2,1,0:T(8,128)} %bitcast.102, bf16[1,256,4096]{2,1,0:T(8,128)(2,1)S(1)} %copy-done.1, bf16[512,4096]{1,0:T(8,128)(2,1)} %reshape.186, bf16[2,4096,256]{2,1,0:T(8,128)(2,1)} %get-tuple-element.12, f32[512,256]{1,0:T(8,128)S(1)} %fusion.9), kind=kOutput, calls=%fused_computation.6 | convolution fusion | flops 2153512960 | bytes 17301504 | tf_op jit(solution)/shard_map/dot_general | solution.py:43
  626.1 7.7 %convert_element_type.179 = bf16[4,64,2,4096]{3,2,1,0:T(2,128)(2,1)} reshape(bf16[512,4096]{1,0:T(8,128)(2,1)} %convolution_convert_fusion.2) | data formatting | bytes 8388608 | tf_op jit(solution)/shard_map/convert_element_type | solution.py:67
  633.8 7.0 copy.42
  640.9 3.3 copy.48
  644.2 7.1 all-to-all-start.3
  651.3 35.9 %reduce-scatter.3.cloned.1.call-done = bf16[1,64,2,4096]{3,1,2,0:T(8,128)(2,1)} async-done(((bf16[4,64,2,4096]{3,1,2,0:T(8,128)(2,1)}), bf16[1,64,2,4096]{3,1,2,0:T(8,128)(2,1)}) %reduce-scatter.3.cloned.1.call-update) | async-done | bytes 1048592 | tf_op jit(solution)/shard_map/reduce_scatter | solution.py:66
  687.1 3.3 copy.43
  690.5 10.8 %all-to-all-start.1 = ((bf16[1,64,2,4096]{3,2,0,1:T(2,128)(2,1)}), bf16[1,64,2,4096]{3,2,0,1:T(2,128)(2,1)S(1)}, u32[]{:S(2)}, u32[]{:S(2)}) async-start(bf16[1,64,2,4096]{3,2,0,1:T(2,128)(2,1)} %copy.43), calls=%async_computation.2 | async-start | bytes 2097152 | tf_op jit(solution)/shard_map/all_to_all | solution.py:69
  703.8 1.2 convolution_convert_fusion.4
  704.9 24.4 %all-to-all-done.1 = bf16[1,64,2,4096]{3,2,0,1:T(2,128)(2,1)S(1)} async-done(((bf16[1,64,2,4096]{3,2,0,1:T(2,128)(2,1)}), bf16[1,64,2,4096]{3,2,0,1:T(2,128)(2,1)S(1)}, u32[]{:S(2)}, u32[]{:S(2)}) %all-to-all-start.1) | async-done | bytes 1048608 | tf_op jit(solution)/shard_map/all_to_all | solution.py:69
  729.8 1.2 convolution_convert_fusion.5
  (73 shorter events, 9.7 us)
Async XLA Ops:
  7.2 695.7 %copy-start = (f32[8,8]{1,0:T(8,128)S(1)}, f32[8,8]{1,0:T(8,128)}, u32[]{:S(2)}) copy-start(f32[8,8]{1,0:T(8,128)} %param.18) | copy-start | bytes 772
  54.1 23.9 %copy-start.1 = (bf16[1,256,4096]{2,1,0:T(8,128)(2,1)S(1)}, bf16[1,256,4096]{2,1,0:T(8,128)(2,1)}, u32[]{:S(2)}) copy-start(bf16[1,256,4096]{2,1,0:T(8,128)(2,1)} %param.24) | copy-start | bytes 6291460
  54.1 24.0 %copy-start.6 = (bf16[1,2,32,2]{2,3,1,0:T(2,128)(2,1)S(1)}, bf16[1,2,32,2]{2,3,1,0:T(2,128)(2,1)}, u32[]{:S(2)}) copy-start(bf16[1,2,32,2]{2,3,1,0:T(2,128)(2,1)} %param.23) | copy-start | bytes 772
  54.1 29.3 %copy-start.7 = (bf16[1,2,32]{2,1,0:T(2,128)(2,1)S(1)}, bf16[1,2,32]{2,1,0:T(2,128)(2,1)}, u32[]{:S(2)}) copy-start(bf16[1,2,32]{2,1,0:T(2,128)(2,1)} %param.25) | copy-start | bytes 388
  54.1 29.4 %copy-start.4 = (s32[8,8]{1,0:T(8,128)S(1)}, s32[8,8]{1,0:T(8,128)}, u32[]{:S(2)}) copy-start(s32[8,8]{1,0:T(8,128)} %param.15) | copy-start | bytes 772
  54.1 39.5 %copy-start.5 = (s32[64]{0:T(128)S(1)}, s32[64]{0:T(128)}, u32[]{:S(2)}) copy-start(s32[64]{0:T(128)} %param.20) | copy-start | bytes 772
  54.1 366.4 %all-to-all-start.2 = ((bf16[4,64,2,4096]{3,2,0,1:T(2,128)(2,1)}), bf16[4,64,2,4096]{3,2,0,1:T(2,128)(2,1)}, u32[]{:S(2)}, u32[]{:S(2)}) async-start(bf16[4,64,2,4096]{3,2,0,1:T(2,128)(2,1)} %copy.44), calls=%async_computation.3 | async-start | bytes 8388608 | tf_op jit(solution)/shard_map/all_to_all | solution.py:96
  72.6 336.1 %collective-permute-start = (bf16[1,2,4096,256]{3,2,1,0:T(8,128)(2,1)}, bf16[1,2,4096,256]{3,2,1,0:T(8,128)(2,1)}, u32[]{:S(2)}, u32[]{:S(2)}) collective-permute-start(bf16[1,2,4096,256]{3,2,1,0:T(8,128)(2,1)} %param.22), channel_id=1, source_target_pairs={{0,128},{128,0},{4,132},{132,4},{8,136},{136,8},{12,140},{140,12},... | collective-permute-start | bytes 12582920 | tf_op jit(solution)/shard_map/ppermute | solution.py:14
  78.0 329.0 %collective-permute-start.2 = (bf16[1,256,4096]{2,1,0:T(8,128)(2,1)S(1)}, bf16[1,256,4096]{2,1,0:T(8,128)(2,1)}, u32[]{:S(2)}, u32[]{:S(2)}) collective-permute-start(bf16[1,256,4096]{2,1,0:T(8,128)(2,1)S(1)} %copy-done.1), channel_id=1, source_target_pairs={{0,128},{128,0},{4,132},{132,4},{8,136},{136,8},{12,140},{140,12},... | collective-permute-start | bytes 6291464 | tf_op jit(solution)/shard_map/ppermute | solution.py:14
  78.2 294.2 %collective-permute-start.1 = (bf16[1,2,32,2]{2,3,1,0:T(2,128)(2,1)S(1)}, bf16[1,2,32,2]{2,3,1,0:T(2,128)(2,1)S(1)}, u32[]{:S(2)}, u32[]{:S(2)}) collective-permute-start(bf16[1,2,32,2]{2,3,1,0:T(2,128)(2,1)S(1)} %copy-done.6), channel_id=1, source_target_pairs={{0,128},{128,0},{4,132},{132,4},{8,136},{136,8},{12,140},{140,12},... | collective-permute-start | bytes 776 | tf_op jit(solution)/shard_map/ppermute | solution.py:14
  83.4 288.4 %collective-permute-start.3 = (bf16[1,2,32]{2,1,0:T(2,128)(2,1)S(1)}, bf16[1,2,32]{2,1,0:T(2,128)(2,1)S(1)}, u32[]{:S(2)}, u32[]{:S(2)}) collective-permute-start(bf16[1,2,32]{2,1,0:T(2,128)(2,1)S(1)} %copy-done.7), channel_id=1, source_target_pairs={{0,128},{128,0},{4,132},{132,4},{8,136},{136,8},{12,140},{140,12},... | collective-permute-start | bytes 392 | tf_op jit(solution)/shard_map/ppermute | solution.py:14
  116.8 10.2 %copy-start.9 = (s32[64]{0:T(128)S(1)}, s32[64]{0:T(128)}, u32[]{:S(2)}) copy-start(s32[64]{0:T(128)} %param.21) | copy-start | bytes 772
  407.0 2.9 copy-start.2
  420.5 170.4 %all-to-all-start = ((bf16[4,64,2,4096]{3,2,0,1:T(2,128)(2,1)}), bf16[4,64,2,4096]{3,2,0,1:T(2,128)(2,1)}, u32[]{:S(2)}, u32[]{:S(2)}) async-start(bf16[4,64,2,4096]{3,2,0,1:T(2,128)(2,1)} %copy.39), calls=%async_computation | async-start | bytes 8388608 | tf_op jit(solution)/shard_map/all_to_all | solution.py:96
  496.0 144.9 %reduce-scatter.5.cloned.1.call-start = ((), (), s32[]{:S(2)}) async-start(), calls=%async_computation.7 | async-start | bytes 5242880 | tf_op jit(solution)/shard_map/reduce_scatter | solution.py:66
  546.4 140.7 %reduce-scatter.3.cloned.1.call-start = ((), (), s32[]{:S(2)}) async-start(), calls=%async_computation.6 | async-start | bytes 5242880 | tf_op jit(solution)/shard_map/reduce_scatter | solution.py:66
  640.8 60.4 %copy-start.3 = (s32[8,8]{1,0:T(8,128)S(1)}, s32[8,8]{1,0:T(8,128)}, u32[]{:S(2)}) copy-start(s32[8,8]{1,0:T(8,128)} %param.16) | copy-start | bytes 772
  640.8 62.3 %copy-start.8 = (f32[8,8]{1,0:T(8,128)S(1)}, f32[8,8]{1,0:T(8,128)}, u32[]{:S(2)}) copy-start(f32[8,8]{1,0:T(8,128)} %param.17) | copy-start | bytes 772
  644.2 46.3 %all-to-all-start.3 = ((bf16[1,64,2,4096]{3,2,0,1:T(2,128)(2,1)}), bf16[1,64,2,4096]{3,2,0,1:T(2,128)(2,1)S(1)}, u32[]{:S(2)}, u32[]{:S(2)}) async-start(bf16[1,64,2,4096]{3,2,0,1:T(2,128)(2,1)} %copy.48), calls=%async_computation.5 | async-start | bytes 2097152 | tf_op jit(solution)/shard_map/all_to_all | solution.py:69
  690.5 38.9 %all-to-all-start.1 = ((bf16[1,64,2,4096]{3,2,0,1:T(2,128)(2,1)}), bf16[1,64,2,4096]{3,2,0,1:T(2,128)(2,1)S(1)}, u32[]{:S(2)}, u32[]{:S(2)}) async-start(bf16[1,64,2,4096]{3,2,0,1:T(2,128)(2,1)} %copy.43), calls=%async_computation.2 | async-start | bytes 2097152 | tf_op jit(solution)/shard_map/all_to_all | solution.py:69
Sparse Core Ops, SparseCore 0:
  546.6 49.7 reduce-scatter.4
  640.9 46.1 reduce-scatter.2
where the time goes:
time: 749 us; the launch traced here: 738 us
  waiting for transfers between devices  348 us (46%)
  local copies, waits for them, and re-layouts  148 us (20%)
  starting transfers between devices  123 us (16%)
  matrix products  40.9 us (5%)
  blocking collectives  40.4 us (5%)
  other arithmetic  22.3 us (3%)
  between operations  15.4 us (2%)
    ppermute x4, waiting for transfers between devices, partner(): return lax.ppermute(block, axis, route)  244 us
    all_to_all x2, starting transfers between devices, decode_step(): lax.all_to_all(outgoing, 'expert', split_axis=1, concat_axis=1, tiled=True)  93.9 us
    all_to_all x2, waiting for transfers between devices, decode_step(): lax.all_to_all(outgoing, 'expert', split_axis=1, concat_axis=1, tiled=True)  44.4 us
    mul x6, local copies, waits for them, and re-layouts, dequantize(): scaled = blocked * scales.astype(jnp.float32)[..., :, None, :, None]  39 us
    reduce_scatter x2, waiting for transfers between devices, finish(): lax.psum_scatter(partial_terms.astype(jnp.bfloat16), 'replica', scatter_d...  35.9 us
    reshape x4, local copies, waits for them, and re-layouts, decode_step(): outgoing.astype(jnp.bfloat16).reshape(copies, experts, capacity, features)  35.8 us
    convert_element_type x4, local copies, waits for them, and re-layouts, finish(): partial_terms.astype(jnp.bfloat16)  29.4 us
    all_to_all x2, waiting for transfers between devices, finish(): lax.all_to_all(summed, 'expert', split_axis=1, concat_axis=1, tiled=True)  24.4 us
  transfers between devices with their start and end apart: 10, of which 4 were waited for; matrix products, arithmetic and copies ran while one was open for 25% of the time, Pallas kernels for 0%

commit v1 on v0

--- a/solution.py
+++ b/solution.py
@@ -78,7 +78,9 @@
     normed = rms_normed(hidden, norm_gain)
     own_picks = pick_slots(routes, owner_slots, experts, capacity)
     pooled, pooled_routes = (
-        lax.all_gather(normed, "replica", axis=0, tiled=True),
+        jnp.concatenate(
+            lax.all_to_all(jnp.stack([normed] * lax.axis_size("replica")), "replica", 0, 0), axis=0
+        ),
         lax.all_gather(routes, "replica", axis=0, tiled=True),
     )
     grouped = pooled_routes.reshape(copies, tokens_here, top_count)

time: 749 us -> 777 us (1.037)
  waiting for transfers between devices: 348 us -> 380 us
  blocking collectives: 40.4 us -> 20.9 us
  other arithmetic: 22.3 us -> 32.2 us
    ppermute x4, waiting for transfers between devices: 244 us -> 275 us  [partner(): return lax.ppermute(block, axis, route)]
    all_gather x2 -> x0, blocking collectives: 19.9 us -> none  [decode_step(): lax.all_gather(normed, 'replica', axis=0, tiled=True)]
    convert_element_type x1, other arithmetic: 10.6 us -> 20.4 us  [dequantize(): return scaled.reshape(values.shape).astype(jnp.bfloat16)]
    all_to_all x0 -> x2, starting transfers between devices: none -> 8.24 us  [decode_step(): lax.all_to_all(jnp.stack([normed] * lax.axis_size('replica')), 'replica',...]
  transfers between devices with their start and end apart: 10 -> 12, of which waited for: 4 -> 4; matrix products, arithmetic and copies ran while one was open for 25% -> 28% of each run, Pallas kernels for 0% -> 0%
where the time goes in v1:
time: 777 us; the launch traced here: 768 us
  waiting for transfers between devices  380 us (49%)
  local copies, waits for them, and re-layouts  149 us (19%)
  starting transfers between devices  129 us (17%)
  matrix products  40.9 us (5%)
  other arithmetic  32.2 us (4%)
  blocking collectives  20.9 us (3%)
  between operations  15.4 us (2%)
    ppermute x4, waiting for transfers between devices, partner(): return lax.ppermute(block, axis, route)  275 us
    all_to_all x2, starting transfers between devices, decode_step(): lax.all_to_all(outgoing, 'expert', split_axis=1, concat_axis=1, tiled=True)  91.5 us
    all_to_all x2, waiting for transfers between devices, decode_step(): lax.all_to_all(outgoing, 'expert', split_axis=1, concat_axis=1, tiled=True)  44.4 us
    mul x6, local copies, waits for them, and re-layouts, dequantize(): scaled = blocked * scales.astype(jnp.float32)[..., :, None, :, None]  39 us
    reduce_scatter x2, waiting for transfers between devices, finish(): lax.psum_scatter(partial_terms.astype(jnp.bfloat16), 'replica', scatter_d...  36.9 us
    reshape x4, local copies, waits for them, and re-layouts, decode_step(): outgoing.astype(jnp.bfloat16).reshape(copies, experts, capacity, features)  35.5 us
    convert_element_type x4, local copies, waits for them, and re-layouts, finish(): partial_terms.astype(jnp.bfloat16)  29.4 us
    all_to_all x2, waiting for transfers between devices, finish(): lax.all_to_all(summed, 'expert', split_axis=1, concat_axis=1, tiled=True)  24.4 us
  transfers between devices with their start and end apart: 12, of which 4 were waited for; matrix products, arithmetic and copies ran while one was open for 28% of the time, Pallas kernels for 0%

profile of v1, /device:TPU:1, one launch (start us, length us, event | category | flops | bytes accessed | tf_op | source)
XLA Modules:
  0.0 767.7 jit_solution(16300633110477485671)
XLA Ops:
  7.2 1.0 fusion.21
  8.2 1.0 fusion.24
  9.2 1.0 fusion.26
  10.9 4.8 all-to-all-start.3
  17.2 10.1 %all_gather.7 = s32[32,8]{1,0:T(8,128)S(1)} all-gather(s32[8,8]{1,0:T(8,128)} %param.16), channel_id=1, replica_groups=mesh['expert'=64,'replica'=4] {'replica'}, dimensions={0}, use_global_device_ids=true | all-gather | bytes 1280 | tf_op jit(solution)/shard_map/all_gather | solution.py:84
  29.5 3.4 all-to-all-start
  32.9 3.3 convolution_convert_fusion.1
  36.2 7.6 reshape.185
  43.8 10.1 %copy.44 = bf16[4,64,2,4096]{3,2,0,1:T(2,128)(2,1)} copy(bf16[4,64,2,4096]{3,2,1,0:T(2,128)(2,1)} %reshape.185) | data formatting | bytes 8388608 | tf_op jit(solution)/shard_map/reshape | solution.py:97
  54.0 16.1 %all-to-all-start.4 = ((bf16[4,64,2,4096]{3,2,0,1:T(2,128)(2,1)}), bf16[4,64,2,4096]{3,2,0,1:T(2,128)(2,1)}, u32[]{:S(2)}, u32[]{:S(2)}) async-start(bf16[4,64,2,4096]{3,2,0,1:T(2,128)(2,1)} %copy.44), calls=%async_computation.5 | async-start | bytes 8388608 | tf_op jit(solution)/shard_map/all_to_all | solution.py:98
  70.1 5.5 collective-permute-start
  75.7 5.3 collective-permute-start.1
  81.1 10.9 %all_gather.6 = s32[32,8]{1,0:T(8,128)S(1)} all-gather(s32[8,8]{1,0:T(8,128)S(1)} %copy-done.4), channel_id=1, replica_groups=mesh['expert'=64,'replica'=4] {'replica'}, dimensions={0}, use_global_device_ids=true | all-gather | bytes 1280 | tf_op jit(solution)/shard_map/all_gather | solution.py:84
  94.7 274.7 %collective-permute-done.3 = bf16[1,2,32]{2,1,0:T(2,128)(2,1)S(1)} collective-permute-done((bf16[1,2,32]{2,1,0:T(2,128)(2,1)S(1)}, bf16[1,2,32]{2,1,0:T(2,128)(2,1)S(1)}, u32[]{:S(2)}, u32[]{:S(2)}) %collective-permute-start.3) | collective-permute-done | bytes 160 | tf_op jit(solution)/shard_map/ppermute | solution.py:14
  370.6 5.4 mul.142
  376.0 11.5 %mul.143 = f32[2,4096,256]{2,1,0:T(8,128)} reshape(f32[2,32,128,2,128]{4,3,2,1,0:T(2,128)} %mul.142) | data formatting | bytes 16777216 | tf_op jit(solution)/shard_map/mul | solution.py:24
  387.6 5.4 mul.158
  393.0 11.5 %mul.159 = f32[2,4096,256]{2,1,0:T(8,128)} reshape(f32[2,32,128,2,128]{4,3,2,1,0:T(2,128)} %mul.158) | data formatting | bytes 16777216 | tf_op jit(solution)/shard_map/mul | solution.py:24
  404.6 3.3 convolution_convert_fusion.3
  407.9 7.6 reshape.182
  415.5 10.2 %copy.39 = bf16[4,64,2,4096]{3,2,0,1:T(2,128)(2,1)} copy(bf16[4,64,2,4096]{3,2,1,0:T(2,128)(2,1)} %reshape.182) | data formatting | bytes 8388608 | tf_op jit(solution)/shard_map/reshape | solution.py:97
  425.6 1.7 broadcast_select_fusion.1
  427.3 1.3 copy-done.2
  428.6 20.4 %fusion = (bf16[2,4096,256]{2,1,0:T(8,128)(2,1)}, bf16[1,2,4096,256]{3,2,1,0:T(8,128)(2,1)}, bf16[2,4096,256]{2,1,0:T(8,128)(2,1)}) fusion(f32[2,4096,256]{2,1,0:T(8,128)} %mul.159, bf16[1,2,4096,256]{3,2,1,0:T(8,128)(2,1)} %collective-permute-done, bf16[1,2,4096,256]{3,2,1,0:T(8,128)(2,1)S(1)} %copy-done.2, pred[]{:T(512)S(6)} %eq.251, f32[2,4096,256]{2,1,0:T(8,128)} %mul.143), kind=kLoop, calls=%fused_computation.1 | loop fusion | flops 14680064 | bytes 37748736 | tf_op jit(solution)/shard_map/convert_element_type | solution.py:25
  449.0 75.4 %all-to-all-start.1 = ((bf16[4,64,2,4096]{3,2,0,1:T(2,128)(2,1)}), bf16[4,64,2,4096]{3,2,0,1:T(2,128)(2,1)}, u32[]{:S(2)}, u32[]{:S(2)}) async-start(bf16[4,64,2,4096]{3,2,0,1:T(2,128)(2,1)} %copy.39), calls=%async_computation.1 | async-start | bytes 8388608 | tf_op jit(solution)/shard_map/all_to_all | solution.py:98
  524.5 9.7 %copy.45 = bf16[4,64,2,4096]{3,2,1,0:T(2,128)(2,1)} copy(bf16[4,64,2,4096]{3,2,0,1:T(2,128)(2,1)} %all-to-all-done.4) | data formatting | bytes 8388608 | tf_op jit(solution)/shard_map/all_to_all | solution.py:98
  534.2 7.2 reshape.186
  541.4 4.1 fusion.6
  545.6 2.6 mul.163
  548.1 11.9 %convolution_convert_fusion = bf16[512,4096]{1,0:T(8,128)(2,1)} fusion(f32[32,8,32,128]{3,2,1,0:T(8,128)} %bitcast.97, bf16[1,256,4096]{2,1,0:T(8,128)(2,1)} %broadcast_select_fusion.1, f32[512,256]{1,0:T(8,128)S(1)} %fusion.6, bf16[512,4096]{1,0:T(8,128)(2,1)} %reshape.186, bf16[2,4096,256]{2,1,0:T(8,128)(2,1)} %get-tuple-element.6), kind=kOutput, calls=%fused_computation.4 | convolution fusion | flops 2153512960 | bytes 17301504 | tf_op jit(solution)/shard_map/dot_general | solution.py:43
  560.0 7.6 convert_element_type.200
  567.7 7.0 copy.47
  575.0 44.3 %all-to-all-done.1 = bf16[4,64,2,4096]{3,2,0,1:T(2,128)(2,1)} async-done(((bf16[4,64,2,4096]{3,2,0,1:T(2,128)(2,1)}), bf16[4,64,2,4096]{3,2,0,1:T(2,128)(2,1)}, u32[]{:S(2)}, u32[]{:S(2)}) %all-to-all-start.1) | async-done | bytes 4194336 | tf_op jit(solution)/shard_map/all_to_all | solution.py:98
  619.4 9.8 %copy.40 = bf16[4,64,2,4096]{3,2,1,0:T(2,128)(2,1)} copy(bf16[4,64,2,4096]{3,2,0,1:T(2,128)(2,1)} %all-to-all-done.1) | data formatting | bytes 8388608 | tf_op jit(solution)/shard_map/all_to_all | solution.py:98
  629.2 7.2 reshape.183
  636.4 4.1 fusion.9
  640.5 2.6 mul.147
  643.0 11.4 %convolution_convert_fusion.2 = bf16[512,4096]{1,0:T(8,128)(2,1)} fusion(f32[32,8,32,128]{3,2,1,0:T(8,128)} %bitcast.98, bf16[1,256,4096]{2,1,0:T(8,128)(2,1)S(1)} %copy-done.1, bf16[512,4096]{1,0:T(8,128)(2,1)} %reshape.183, bf16[2,4096,256]{2,1,0:T(8,128)(2,1)} %get-tuple-element.12, f32[512,256]{1,0:T(8,128)S(1)} %fusion.9), kind=kOutput, calls=%fused_computation.6 | convolution fusion | flops 2153512960 | bytes 17301504 | tf_op jit(solution)/shard_map/dot_general | solution.py:43
  654.4 7.6 convert_element_type.179
  662.1 7.1 copy.42
  669.2 3.3 copy.48
  672.5 7.1 all-to-all-start.5
  679.6 36.9 %reduce-scatter.3.cloned.1.call-done = bf16[1,64,2,4096]{3,1,2,0:T(8,128)(2,1)} async-done(((bf16[4,64,2,4096]{3,1,2,0:T(8,128)(2,1)}), bf16[1,64,2,4096]{3,1,2,0:T(8,128)(2,1)}) %reduce-scatter.3.cloned.1.call-update) | async-done | bytes 1048592 | tf_op jit(solution)/shard_map/reduce_scatter | solution.py:66
  716.5 3.4 copy.43
  719.9 10.7 %all-to-all-start.2 = ((bf16[1,64,2,4096]{3,2,0,1:T(2,128)(2,1)}), bf16[1,64,2,4096]{3,2,0,1:T(2,128)(2,1)S(1)}, u32[]{:S(2)}, u32[]{:S(2)}) async-start(bf16[1,64,2,4096]{3,2,0,1:T(2,128)(2,1)} %copy.43), calls=%async_computation.3 | async-start | bytes 2097152 | tf_op jit(solution)/shard_map/all_to_all | solution.py:69
  733.2 1.2 convolution_convert_fusion.4
  734.4 24.4 %all-to-all-done.2 = bf16[1,64,2,4096]{3,2,0,1:T(2,128)(2,1)S(1)} async-done(((bf16[1,64,2,4096]{3,2,0,1:T(2,128)(2,1)}), bf16[1,64,2,4096]{3,2,0,1:T(2,128)(2,1)S(1)}, u32[]{:S(2)}, u32[]{:S(2)}) %all-to-all-start.2) | async-done | bytes 1048608 | tf_op jit(solution)/shard_map/all_to_all | solution.py:69
  759.2 1.2 convolution_convert_fusion.5
  (77 shorter events, 11.3 us)
Async XLA Ops:
  7.2 725.1 %copy-start = (f32[8,8]{1,0:T(8,128)S(1)}, f32[8,8]{1,0:T(8,128)}, u32[]{:S(2)}) copy-start(f32[8,8]{1,0:T(8,128)} %param.18) | copy-start | bytes 772
  10.9 17.9 %all-to-all-start.3 = ((bf16[4,8,4096]{2,1,0:T(8,128)(2,1)}), bf16[4,8,4096]{2,1,0:T(8,128)(2,1)S(1)}, u32[]{:S(2)}, u32[]{:S(2)}) async-start(bf16[4,8,4096]{2,1,0:T(8,128)(2,1)} %stack.5), calls=%async_computation.4 | async-start | bytes 524288 | tf_op jit(solution)/shard_map/all_to_all | solution.py:82
  29.5 24.5 %all-to-all-start = ((bf16[4,8,4096]{2,1,0:T(8,128)(2,1)}), bf16[4,8,4096]{2,1,0:T(8,128)(2,1)S(1)}, u32[]{:S(2)}, u32[]{:S(2)}) async-start(bf16[4,8,4096]{2,1,0:T(8,128)(2,1)} %stack.4), calls=%async_computation | async-start | bytes 524288 | tf_op jit(solution)/shard_map/all_to_all | solution.py:82
  54.0 21.6 %copy-start.1 = (bf16[1,256,4096]{2,1,0:T(8,128)(2,1)S(1)}, bf16[1,256,4096]{2,1,0:T(8,128)(2,1)}, u32[]{:S(2)}) copy-start(bf16[1,256,4096]{2,1,0:T(8,128)(2,1)} %param.24) | copy-start | bytes 6291460
  54.0 21.7 %copy-start.6 = (bf16[1,2,32,2]{2,3,1,0:T(2,128)(2,1)S(1)}, bf16[1,2,32,2]{2,3,1,0:T(2,128)(2,1)}, u32[]{:S(2)}) copy-start(bf16[1,2,32,2]{2,3,1,0:T(2,128)(2,1)} %param.23) | copy-start | bytes 772
  54.0 27.0 %copy-start.7 = (bf16[1,2,32]{2,1,0:T(2,128)(2,1)S(1)}, bf16[1,2,32]{2,1,0:T(2,128)(2,1)}, u32[]{:S(2)}) copy-start(bf16[1,2,32]{2,1,0:T(2,128)(2,1)} %param.25) | copy-start | bytes 388
  54.0 27.1 %copy-start.4 = (s32[8,8]{1,0:T(8,128)S(1)}, s32[8,8]{1,0:T(8,128)}, u32[]{:S(2)}) copy-start(s32[8,8]{1,0:T(8,128)} %param.15) | copy-start | bytes 772
  54.0 38.0 %copy-start.5 = (s32[64]{0:T(128)S(1)}, s32[64]{0:T(128)}, u32[]{:S(2)}) copy-start(s32[64]{0:T(128)} %param.20) | copy-start | bytes 772
  54.0 39.3 %copy-start.9 = (s32[64]{0:T(128)S(1)}, s32[64]{0:T(128)}, u32[]{:S(2)}) copy-start(s32[64]{0:T(128)} %param.21) | copy-start | bytes 772
  54.0 395.0 %all-to-all-start.4 = ((bf16[4,64,2,4096]{3,2,0,1:T(2,128)(2,1)}), bf16[4,64,2,4096]{3,2,0,1:T(2,128)(2,1)}, u32[]{:S(2)}, u32[]{:S(2)}) async-start(bf16[4,64,2,4096]{3,2,0,1:T(2,128)(2,1)} %copy.44), calls=%async_computation.5 | async-start | bytes 8388608 | tf_op jit(solution)/shard_map/all_to_all | solution.py:98
  70.1 357.2 %collective-permute-start = (bf16[1,2,4096,256]{3,2,1,0:T(8,128)(2,1)}, bf16[1,2,4096,256]{3,2,1,0:T(8,128)(2,1)}, u32[]{:S(2)}, u32[]{:S(2)}) collective-permute-start(bf16[1,2,4096,256]{3,2,1,0:T(8,128)(2,1)} %param.22), channel_id=1, source_target_pairs={{0,128},{128,0},{4,132},{132,4},{8,136},{136,8},{12,140},{140,12},... | collective-permute-start | bytes 12582920 | tf_op jit(solution)/shard_map/ppermute | solution.py:14
  75.6 350.0 %collective-permute-start.2 = (bf16[1,256,4096]{2,1,0:T(8,128)(2,1)S(1)}, bf16[1,256,4096]{2,1,0:T(8,128)(2,1)}, u32[]{:S(2)}, u32[]{:S(2)}) collective-permute-start(bf16[1,256,4096]{2,1,0:T(8,128)(2,1)S(1)} %copy-done.1), channel_id=1, source_target_pairs={{0,128},{128,0},{4,132},{132,4},{8,136},{136,8},{12,140},{140,12},... | collective-permute-start | bytes 6291464 | tf_op jit(solution)/shard_map/ppermute | solution.py:14
  75.7 294.2 %collective-permute-start.1 = (bf16[1,2,32,2]{2,3,1,0:T(2,128)(2,1)S(1)}, bf16[1,2,32,2]{2,3,1,0:T(2,128)(2,1)S(1)}, u32[]{:S(2)}, u32[]{:S(2)}) collective-permute-start(bf16[1,2,32,2]{2,3,1,0:T(2,128)(2,1)S(1)} %copy-done.6), channel_id=1, source_target_pairs={{0,128},{128,0},{4,132},{132,4},{8,136},{136,8},{12,140},{140,12},... | collective-permute-start | bytes 776 | tf_op jit(solution)/shard_map/ppermute | solution.py:14
  81.0 288.4 %collective-permute-start.3 = (bf16[1,2,32]{2,1,0:T(2,128)(2,1)S(1)}, bf16[1,2,32]{2,1,0:T(2,128)(2,1)S(1)}, u32[]{:S(2)}, u32[]{:S(2)}) collective-permute-start(bf16[1,2,32]{2,1,0:T(2,128)(2,1)S(1)} %copy-done.7), channel_id=1, source_target_pairs={{0,128},{128,0},{4,132},{132,4},{8,136},{136,8},{12,140},{140,12},... | collective-permute-start | bytes 392 | tf_op jit(solution)/shard_map/ppermute | solution.py:14
  425.6 2.9 copy-start.2
  449.0 170.3 %all-to-all-start.1 = ((bf16[4,64,2,4096]{3,2,0,1:T(2,128)(2,1)}), bf16[4,64,2,4096]{3,2,0,1:T(2,128)(2,1)}, u32[]{:S(2)}, u32[]{:S(2)}) async-start(bf16[4,64,2,4096]{3,2,0,1:T(2,128)(2,1)} %copy.39), calls=%async_computation.1 | async-start | bytes 8388608 | tf_op jit(solution)/shard_map/all_to_all | solution.py:98
  524.5 144.8 %reduce-scatter.5.cloned.1.call-start = ((), (), s32[]{:S(2)}) async-start(), calls=%async_computation.9 | async-start | bytes 5242880 | tf_op jit(solution)/shard_map/reduce_scatter | solution.py:66
  574.7 141.8 %reduce-scatter.3.cloned.1.call-start = ((), (), s32[]{:S(2)}) async-start(), calls=%async_computation.8 | async-start | bytes 5242880 | tf_op jit(solution)/shard_map/reduce_scatter | solution.py:66
  669.2 61.5 %copy-start.3 = (s32[8,8]{1,0:T(8,128)S(1)}, s32[8,8]{1,0:T(8,128)}, u32[]{:S(2)}) copy-start(s32[8,8]{1,0:T(8,128)} %param.16) | copy-start | bytes 772
  669.2 63.3 %copy-start.8 = (f32[8,8]{1,0:T(8,128)S(1)}, f32[8,8]{1,0:T(8,128)}, u32[]{:S(2)}) copy-start(f32[8,8]{1,0:T(8,128)} %param.17) | copy-start | bytes 772
  672.5 47.4 %all-to-all-start.5 = ((bf16[1,64,2,4096]{3,2,0,1:T(2,128)(2,1)}), bf16[1,64,2,4096]{3,2,0,1:T(2,128)(2,1)S(1)}, u32[]{:S(2)}, u32[]{:S(2)}) async-start(bf16[1,64,2,4096]{3,2,0,1:T(2,128)(2,1)} %copy.48), calls=%async_computation.7 | async-start | bytes 2097152 | tf_op jit(solution)/shard_map/all_to_all | solution.py:69
  719.9 38.9 %all-to-all-start.2 = ((bf16[1,64,2,4096]{3,2,0,1:T(2,128)(2,1)}), bf16[1,64,2,4096]{3,2,0,1:T(2,128)(2,1)S(1)}, u32[]{:S(2)}, u32[]{:S(2)}) async-start(bf16[1,64,2,4096]{3,2,0,1:T(2,128)(2,1)} %copy.43), calls=%async_computation.3 | async-start | bytes 2097152 | tf_op jit(solution)/shard_map/all_to_all | solution.py:69
Sparse Core Ops, SparseCore 0:
  574.9 50.8 reduce-scatter.4
  669.3 47.1 reduce-scatter.2
